TPU v7x, 32 devices: a whole 2x2x4 slice. The times are simulated.
32 devices in a mesh: grp: 2 (over x), chol: 16 (over z, y, core).
Axes of the slice: x: 2, y: 2, z: 4, core: 2. Of those that a mesh axis runs over, the one named last changes fastest.
Arguments:
- walkers: bfloat16 [1024, 64, 256], P(('grp', 'chol')), parts along dimension 0, may hold values from -6 to 6
- fields: bfloat16 [1024, 1024], P(('grp', 'chol')), parts along dimension 0, may hold values from -6 to 6
- chol_vectors: bfloat16 [1024, 256, 256], P(None, 'chol'), may hold values from -0.375 to 0.375
- rotated: bfloat16 [1024, 64, 256], P(None, 'chol'), may hold values from -0.046875 to 0.046875
- send_walker: int32 [32, 16, 2], P(('grp', 'chol')), parts along dimension 0, may hold values from -1 to 31, as said below
- slot_row: int32 [1024], P(('grp', 'chol')), parts along dimension 0, may hold values from 0 to 31, as said below
Outputs:
- new_walkers: bfloat16 [1024, 64, 256], P(('grp', 'chol')), parts along dimension 0
- force_bias: float32 [1024, 1024], P(('grp', 'chol')), parts along dimension 0
There are 2 independent parts, one for each index of `grp`. A program takes and returns all parts, laid end to end along the dimension named above; an argument that names none is the same for every part. Nothing has to cross between parts.
Inputs may be any that keep to these rules, and one draw needn't show every extreme that they name: `send_walker`: entry [s, d, c] is the index, among the 32 walkers of block s, of the walker that block s sends as its c-th one to block d, or -1 where it sends none; indices of one [s, d] row come first, -1 after. Some pair of blocks uses all 2 entries. `slot_row`: for every slot of block d, s * 2 + c names a valid entry [s, d, c] of send_walker, and every valid entry is named by exactly one slot of block d.
All inputs are finite; a program needn't handle non-finite values.
Results may differ from a plain program's by a relative error of at most 0.0075.
Values may be sent and summed in bfloat16 or wider, within the bound.
A program may use at most 64 MiB of HBM per device.

v0:
```python
import functools
import math

import jax
import jax.numpy as jnp
from jax import lax
from jax.experimental import pallas as pl
from jax.experimental.pallas import tpu as pltpu
from jax.sharding import PartitionSpec as P

field_scale = 1.5
chunk_slots = 16
degrees = 5
unfold_depth = 64
MESH = pl.DeviceIdType.MESH


def stride_of(blocks):
    return next(h for h in (7, 5, 3, 1) if math.gcd(h, blocks) == 1)


def unfold(source, scratch, target):
    depth, rows, orbitals = source.shape
    step = scratch.shape[1] // rows

    def body(b, carry):
        first = pl.multiple_of(b * step, step)
        block = source[pl.ds(first, step)].astype(jnp.float32).reshape(step * rows, orbitals)
        for h in range(orbitals // 128):
            scratch[h] = block[:, h * 128 : (h + 1) * 128]
        for r in range(rows):
            for h in range(orbitals // 128):
                low = r * orbitals + h * 128
                target[pl.ds(first, step), low : low + 128] = scratch[
                    h, pl.ds(r, step, stride=rows), :
                ].astype(jnp.bfloat16)
        return carry

    lax.fori_loop(0, depth // step, body, 0)


def exchange(me, blocks, send, recv, chunk, send_sem, recv_sem, place=lambda d: d, land=lambda d: d):
    hop = stride_of(blocks)

    def step(k, carry):
        peer = lax.rem(me + k * hop, blocks)
        pltpu.make_async_remote_copy(
            src_ref=send.at[chunk, place(peer)],
            dst_ref=recv.at[chunk, land(me)],
            send_sem=send_sem.at[chunk],
            recv_sem=recv_sem.at[chunk],
            device_id={"chol": peer},
            device_id_type=MESH,
        ).start()
        return carry

    lax.fori_loop(1, blocks, step, 0)
    recv[chunk, land(me)] = send[chunk, place(me)]


def arrived(blocks, recv, chunk, sem):
    whole = recv.at[chunk, pl.ds(0, blocks - 1)]
    pltpu.make_async_copy(whole, whole, sem.at[chunk]).wait()


def kernel(
    dims,
    send_walker,
    slot_row,
    walkers,
    fields,
    chol_hbm,
    rotated_raw,
    new_walkers,
    force_bias,
    chol_raw,
    chol_wide,
    chol,
    rotated_wide,
    rotated,
    all_fields,
    br_send,
    br_recv,
    op_send,
    op_recv,
    op_rows,
    totals,
    nw_send,
    nw_recv,
    pair_send,
    pair_recv,
    pair_own,
    fb_send,
    fb_recv,
    send_sems,
    recv_sems,
    field_sems,
    load_sem,
    op_sems,
):
    blocks, chunks, width, cap, rows, elec = dims
    slots, electrons, orbitals = walkers.shape
    nchol = rotated.shape[0]
    halves = orbitals // 128
    me = lax.axis_index("chol")
    pairs = blocks // 2
    core, pair = lax.rem(me, 2), me // 2
    groups = math.gcd(4, blocks)
    share_of = blocks // groups
    hop = stride_of(blocks)
    load = pltpu.make_async_copy(chol_hbm, chol_raw, load_sem)
    load.start()

    barrier = pltpu.get_barrier_semaphore()

    def greet(k, carry):
        pl.semaphore_signal(
            barrier, inc=1, device_id={"chol": lax.rem(me + k, blocks)}, device_id_type=MESH
        )
        return carry

    lax.fori_loop(1, blocks, greet, 0)

    def pick(d, carry):
        for c in range(cap):
            br_send[0, d, c] = walkers[jnp.maximum(send_walker[d * cap + c], 0)]
        return carry

    lax.fori_loop(0, blocks, pick, 0)
    pl.semaphore_wait(barrier, blocks - 1)

    def share(k, carry):
        pltpu.make_async_remote_copy(
            src_ref=fields,
            dst_ref=all_fields.at[core, pair],
            send_sem=field_sems.at[0],
            recv_sem=field_sems.at[1],
            device_id={"chol": lax.rem(pair + k, pairs) * 2 + core},
            device_id_type=MESH,
        ).start()
        return carry

    lax.fori_loop(1, pairs, share, 0)
    all_fields[core, pair] = fields[...]
    load.wait()
    unfold(chol_raw, chol_wide, chol)
    same_core = all_fields.at[core, pl.ds(0, pairs - 1)]
    pltpu.make_async_copy(same_core, same_core, field_sems.at[1]).wait()
    across = pltpu.make_async_remote_copy(
        src_ref=all_fields.at[core],
        dst_ref=all_fields.at[core],
        send_sem=field_sems.at[2],
        recv_sem=field_sems.at[3],
        device_id={"chol": pair * 2 + 1 - core},
        device_id_type=MESH,
    )
    across.start()
    exchange(me, blocks, br_send, br_recv, 0, send_sems.at[0], recv_sems.at[0])

    across.wait_recv()
    scale = field_scale / math.sqrt(nchol)
    cols = rows * orbitals
    tile = min(512, cols)

    @pl.loop(0, cols // tile)
    def _(n):
        at = pl.ds(pl.multiple_of(n * tile, tile), tile)
        left = all_fields[...].reshape(blocks * slots, nchol)
        part = jnp.dot(left, chol[:, at], preferred_element_type=jnp.float32) * scale
        part = part.astype(jnp.bfloat16).reshape(blocks, chunks, width, tile)
        for q in range(chunks):
            op_send[q, :, :, at] = part[:, q]

    def send_operators(q):
        for group in range(groups):
            def step(k, carry):
                peer = lax.rem(me + k * hop, blocks)
                pltpu.make_async_remote_copy(
                    src_ref=op_send.at[q, place(peer)],
                    dst_ref=op_recv.at[q, me],
                    send_sem=send_sems.at[1, q],
                    recv_sem=op_sems.at[q, group],
                    device_id={"chol": peer},
                    device_id_type=MESH,
                ).start()
                return carry

            lax.fori_loop(max(1, group * share_of), (group + 1) * share_of, step, 0)
        op_recv[q, me] = op_send[q, place(me)]

    def place(d):
        return lax.rem(d, 2) * pairs + d // 2

    def taylor(q):
        def spread(k, carry):
            s = lax.rem(me + (blocks - k) * hop, blocks)
            block = op_recv[q, s].astype(jnp.float32)
            for r in range(rows):
                for h in range(halves):
                    low = r * orbitals + h * 128
                    op_rows[h, pl.ds(s * rows + r, width, stride=orbitals), :] = block[
                        :, low : low + 128
                    ]
            return carry

        for group in range(groups):
            count = share_of - 1 if group == 0 else share_of
            whole = op_recv.at[q, pl.ds(0, count)]
            pltpu.make_async_copy(whole, whole, op_sems.at[q, group]).wait()
            lax.fori_loop(group * share_of, (group + 1) * share_of, spread, 0)
        group = 4

        @pl.loop(0, width // group)
        def _(g):
            ops, terms, sums = [], [], []
            for u in range(group):
                w = g * group + u
                first = pl.ds(pl.multiple_of(w * orbitals, orbitals), orbitals)
                ops.append(
                    jnp.concatenate([op_rows[h, first, :] for h in range(halves)], axis=1).astype(
                        jnp.bfloat16
                    )
                )
                row = slot_row[q * width + w]
                terms.append(br_recv[0, row // cap, row % cap])
                sums.append(terms[u].astype(jnp.float32))
            for degree in range(1, degrees + 1):
                for u in range(group):
                    product = lax.dot_general(
                        terms[u],
                        ops[u],
                        (((1,), (1,)), ((), ())),
                        preferred_element_type=jnp.float32,
                    )
                    terms[u] = (product * (1.0 / degree)).astype(jnp.bfloat16)
                    sums[u] = sums[u] + terms[u].astype(jnp.float32)
            for u in range(group):
                w = g * group + u
                new_walkers[q * width + w] = sums[u].astype(jnp.bfloat16)
                place = pl.ds(pl.multiple_of(w * electrons, electrons), electrons)
                for h in range(halves):
                    totals[h, place, :] = sums[u][:, h * 128 : (h + 1) * 128]

        def turn(d, carry):
            for e in range(elec):
                for h in range(halves):
                    low = e * orbitals + h * 128
                    nw_send[q, d, :, low : low + 128] = totals[
                        h, pl.ds(d * elec + e, width, stride=electrons), :
                    ].astype(jnp.bfloat16)
            return carry

        lax.fori_loop(0, blocks, turn, 0)
        exchange(me, blocks, nw_send, nw_recv, q, send_sems.at[2], recv_sems.at[2], land=place)

    def partial(q, half, target):
        left = nw_recv[q, pl.ds(half * pairs, pairs)].reshape(pairs * width, elec * orbitals)
        step = min(256, nchol)

        @pl.loop(0, nchol // step)
        def _(n):
            at = pl.ds(pl.multiple_of(n * step, step), step)
            target[:, at] = lax.dot_general(
                left, rotated[at, :], (((1,), (1,)), ((), ())), preferred_element_type=jnp.float32
            )

    def bias(q):
        partial(q, 1 - core, pair_send.at[q])
        across = pltpu.make_async_remote_copy(
            src_ref=pair_send.at[q],
            dst_ref=pair_recv.at[q],
            send_sem=send_sems.at[4, q],
            recv_sem=recv_sems.at[4, q],
            device_id={"chol": pair * 2 + 1 - core},
            device_id_type=MESH,
        )
        across.start()
        partial(q, core, pair_own)
        across.wait_recv()
        both = (pair_own[...] + pair_recv[q]).astype(jnp.bfloat16)
        fb_send[q] = both.reshape(pairs, width, nchol)

        def step(k, carry):
            peer = lax.rem(pair + k, pairs)
            pltpu.make_async_remote_copy(
                src_ref=fb_send.at[q, peer],
                dst_ref=fb_recv.at[q, pair],
                send_sem=send_sems.at[3, q],
                recv_sem=recv_sems.at[3, q],
                device_id={"chol": peer * 2 + core},
                device_id_type=MESH,
            ).start()
            return carry

        lax.fori_loop(1, pairs, step, 0)
        fb_recv[q, pair] = fb_send[q, pair]

    def finish(q):
        force_bias[q * width : (q + 1) * width, :] = lax.fori_loop(
            1,
            pairs,
            lambda s, acc: acc + fb_recv[q, s].astype(jnp.float32),
            fb_recv[q, 0].astype(jnp.float32),
        )

    for q in range(min(2, chunks)):
        send_operators(q)
    unfold(rotated_raw, rotated_wide, rotated)
    arrived(blocks, br_recv, 0, recv_sems.at[0])
    for q in range(chunks + 2):
        if q < chunks:
            if q + 2 < chunks:
                send_operators(q + 2)
            taylor(q)
        if 1 <= q <= chunks:
            arrived(blocks, nw_recv, q - 1, recv_sems.at[2])
            bias(q - 1)
        if q >= 2:
            arrived(pairs, fb_recv, q - 2, recv_sems.at[3])
            finish(q - 2)
    arrived(blocks, br_send, 0, send_sems.at[0])
    across.wait_send()
    pltpu.make_async_copy(same_core, same_core, field_sems.at[0]).wait()
    for q in range(chunks):
        arrived(blocks, op_send, q, send_sems.at[1])
        arrived(blocks, nw_send, q, send_sems.at[2])
        arrived(pairs, fb_send, q, send_sems.at[3])
        pltpu.make_async_copy(pair_send.at[q], pair_send.at[q], send_sems.at[4, q]).wait()


def shards(blocks, walkers, fields, chol_vectors, rotated, send_walker, slot_row):
    slots, electrons, orbitals = walkers.shape
    nchol, rows, _ = chol_vectors.shape
    elec = rotated.shape[1]
    cap = send_walker.shape[-1]
    width = min(chunk_slots, slots)
    chunks = slots // width
    dims = (blocks, chunks, width, cap, rows, elec)
    bf16, f32 = jnp.bfloat16, jnp.float32
    vmem, smem = (pl.BlockSpec(memory_space=m) for m in (pltpu.VMEM, pltpu.SMEM))
    return pl.pallas_call(
        functools.partial(kernel, dims),
        out_shape=(
            jax.ShapeDtypeStruct(walkers.shape, bf16),
            jax.ShapeDtypeStruct((slots, nchol), f32),
        ),
        in_specs=[smem, smem, vmem, vmem, pl.BlockSpec(memory_space=pl.ANY), vmem],
        out_specs=(vmem, vmem),
        scratch_shapes=[
            pltpu.VMEM(chol_vectors.shape, bf16),
            pltpu.VMEM((orbitals // 128, rows * unfold_depth, 128), f32),
            pltpu.VMEM((nchol, rows * orbitals), bf16),
            pltpu.VMEM((orbitals // 128, elec * unfold_depth, 128), f32),
            pltpu.VMEM((nchol, elec * orbitals), bf16),
            pltpu.VMEM((2, blocks // 2, slots, nchol), bf16),
            pltpu.VMEM((1, blocks, cap, electrons, orbitals), bf16),
            pltpu.VMEM((1, blocks, cap, electrons, orbitals), bf16),
            pltpu.VMEM((chunks, blocks, width, rows * orbitals), bf16),
            pltpu.VMEM((chunks, blocks, width, rows * orbitals), bf16),
            pltpu.VMEM((orbitals // 128, width * orbitals, 128), f32),
            pltpu.VMEM((orbitals // 128, width * electrons, 128), f32),
            pltpu.VMEM((chunks, blocks, width, elec * orbitals), bf16),
            pltpu.VMEM((chunks, blocks, width, elec * orbitals), bf16),
            pltpu.VMEM((chunks, blocks // 2 * width, nchol), f32),
            pltpu.VMEM((chunks, blocks // 2 * width, nchol), f32),
            pltpu.VMEM((blocks // 2 * width, nchol), f32),
            pltpu.VMEM((chunks, blocks // 2, width, nchol), bf16),
            pltpu.VMEM((chunks, blocks // 2, width, nchol), bf16),
            pltpu.SemaphoreType.DMA((5, chunks)),
            pltpu.SemaphoreType.DMA((5, chunks)),
            pltpu.SemaphoreType.DMA((4,)),
            pltpu.SemaphoreType.DMA,
            pltpu.SemaphoreType.DMA((chunks, math.gcd(4, blocks))),
        ],
        compiler_params=pltpu.CompilerParams(
            collective_id=0, has_side_effects=True, vmem_limit_bytes=60 * 1024 * 1024
        ),
    )(
        send_walker.reshape(-1),
        slot_row,
        walkers,
        fields,
        chol_vectors,
        rotated,
    )


def solution(mesh):
    in_specs = (
        P(("grp", "chol"), None, None),
        P(("grp", "chol"), None),
        P(None, "chol", None),
        P(None, "chol", None),
        P(("grp", "chol"), None, None),
        P(("grp", "chol")),
    )
    out_specs = (P(("grp", "chol"), None, None), P(("grp", "chol"), None))
    return jax.shard_map(
        functools.partial(shards, mesh.shape["chol"]),
        mesh=mesh,
        in_specs=in_specs,
        out_specs=out_specs,
        check_vma=False,
    )
```

profile of v0, /device:TPU:0, one launch (start us, length us, event | category | flops | bytes accessed | tf_op | source)
XLA Modules:
  0.0 174.1 jit_solution(11486143684339101651)
XLA Ops:
  0.6 0.8 copy.9
  1.4 0.6 reshape.7.send_walker
  2.0 168.3 %shard_map.77 = (bf16[32,64,256]{2,1,0:T(8,128)(2,1)}, f32[32,1024]{1,0:T(8,128)}) custom-call(s32[32]{0:T(128)} %reshape.7.send_walker, s32[32]{0:T(128)} %slot_row.1, bf16[32,64,256]{2,1,0:T(8,128)(2,1)} %walkers.1, bf16[32,1024]{1,0:T(8,128)(2,1)} %fields.1, bf16[1024,16,256]{2,1,0:T(8,128)(2,1)} %chol_hbm.1, bf16[1024,4,256]{2,1,0:T(4,128)(2,1)} %rotated_raw.1), custom_call_target="tpu_custom_call" | custom-call | tf_op jit(solution)/shard_map/pallas_call | solution.py:341
  170.3 2.3 %copy.12 = bf16[32,64,256]{2,1,0:T(8,128)(2,1)} copy(bf16[32,64,256]{2,1,0:T(8,128)(2,1)} %get-tuple-element.4) | data formatting | bytes 2097152
  172.6 1.6 copy.13
where the time goes:
time: 174 us
  Pallas kernels  168 us (97%)
  local copies, waits for them, and re-layouts  5.23 us (3%)
    pallas_call x1, Pallas kernels, shards(): pl.pallas_call(functools.partial(kernel, dims), out_shape=(jax.ShapeDtype...  168 us
    unnamed x3, local copies, waits for them, and re-layouts  4.63 us

commit v1 on v0

--- a/solution.py
+++ b/solution.py
@@ -385,6 +385,570 @@
     )
 
 
+def strided_relay(source, scratch, target, start, count):
+    rows, orbitals = source.shape[1:]
+    step = min(scratch.shape[1] // rows, count)
+
+    def body(b, carry):
+        first = pl.multiple_of(start + b * step, step)
+        block = source[pl.ds(first, step)].astype(jnp.float32).reshape(step * rows, orbitals)
+        for h in range(orbitals // 128):
+            scratch[h, : step * rows] = block[:, h * 128 : (h + 1) * 128]
+        for r in range(rows):
+            for h in range(orbitals // 128):
+                low = r * orbitals + h * 128
+                target[pl.ds(first, step), low : low + 128] = scratch[
+                    h, pl.ds(r, step, stride=rows), :
+                ].astype(jnp.bfloat16)
+        return carry
+
+    lax.fori_loop(0, count // step, body, 0)
+
+
+def parent_kernel(
+    dims,
+    send_walker,
+    slot_row,
+    fields,
+    walkers_hbm,
+    chol_hbm,
+    rotated_hbm,
+    new_walkers,
+    force_bias,
+    walkers,
+    chol_raw,
+    chol_wide,
+    chol,
+    rotated_raw,
+    rotated_wide,
+    rotated,
+    all_fields,
+    left,
+    op_wide,
+    op_send,
+    op_recv,
+    totals,
+    nw_full,
+    nw_send,
+    nw_recv,
+    part,
+    pair_recv,
+    fb_send,
+    fb_recv,
+    fb_total,
+    fw_wide,
+    fw_send,
+    fw_recv,
+    fw_rows,
+    branch,
+    load_sems,
+    field_send,
+    field_core,
+    field_line,
+    field_row,
+    op_sent,
+    op_got,
+    nw_sent,
+    nw_got,
+    br_sent,
+    br_got,
+    pair_sent,
+    pair_got,
+    fb_sent,
+    fb_got,
+    fw_sent,
+    fw_got,
+):
+    blocks, cap, rows, elec = dims
+    slots, nchol = fields.shape
+    electrons, orbitals = walkers.shape[1:]
+    halves = orbitals // 128
+    me = lax.axis_index("chol")
+    pairs, lines, half = blocks // 2, blocks // 4, blocks // 2
+    core, pair = lax.rem(me, 2), me // 2
+    line, across = pair // 2, lax.rem(pair, 2)
+    side, local = me // half, lax.rem(me, half)
+    away = 1 - side
+    near = electrons // 2
+    bf16, f32 = jnp.bfloat16, jnp.float32
+
+    def wait(ref, sem):
+        pltpu.make_async_copy(ref, ref, sem).wait()
+
+    def send(src, dst, sent, got, peer):
+        pltpu.make_async_remote_copy(
+            src_ref=src,
+            dst_ref=dst,
+            send_sem=sent,
+            recv_sem=got,
+            device_id={"chol": peer},
+            device_id_type=MESH,
+        ).start()
+
+    def far_then_near(far, close):
+        def first(t, carry):
+            far(away * half + lax.rem(local + t, half))
+            return carry
+
+        def second(t, carry):
+            close(side * half + lax.rem(local + t, half))
+            return carry
+
+        lax.fori_loop(0, half, first, 0)
+        lax.fori_loop(1, half, second, 0)
+
+    def row_of(d):
+        return lax.rem(d, 2) * pairs + d // 2
+
+    pieces = 4
+    span = nchol // pieces
+    chol_loads = [
+        pltpu.make_async_copy(
+            chol_hbm.at[pl.ds(p * span, span)], chol_raw.at[pl.ds(p * span, span)], load_sems.at[p]
+        )
+        for p in range(pieces)
+    ]
+    for load in chol_loads:
+        load.start()
+    walker_load = pltpu.make_async_copy(walkers_hbm, walkers, load_sems.at[pieces])
+    rotated_load = pltpu.make_async_copy(rotated_hbm, rotated_raw, load_sems.at[pieces + 1])
+    walker_load.start()
+    rotated_load.start()
+
+    barrier = pltpu.get_barrier_semaphore()
+
+    def greet(k, carry):
+        pl.semaphore_signal(
+            barrier, inc=1, device_id={"chol": lax.rem(me + k, blocks)}, device_id_type=MESH
+        )
+        return carry
+
+    lax.fori_loop(1, blocks, greet, 0)
+
+    order = lax.broadcasted_iota(jnp.int32, (slots, slots), 0)
+    place = lax.broadcasted_iota(jnp.int32, (slots, slots), 1)
+    chosen = jnp.zeros((slots, slots), f32)
+    for p in range(slots):
+        entry = slot_row[p]
+        target = lax.rem(entry, cap) * blocks + entry // cap
+        chosen = jnp.where((place == p) & (order == target), 1.0, chosen)
+    all_fields[pair, core] = jnp.dot(
+        chosen.astype(bf16), fields[...], preferred_element_type=f32
+    ).astype(bf16)
+
+    for p in range(pieces):
+        chol_loads[p].wait()
+        strided_relay(chol_raw, chol_wide, chol, p * span, span)
+
+    scale = field_scale / math.sqrt(nchol)
+    cols = rows * orbitals
+    tile = min(512, cols)
+    deep = tile // orbitals
+
+    def operators(m):
+        @pl.loop(0, cols // tile)
+        def _(n):
+            at = pl.ds(pl.multiple_of(n * tile, tile), tile)
+            out = jnp.dot(left[:m], chol[:, at], preferred_element_type=f32) * scale
+            for i in range(deep):
+                for h in range(halves):
+                    low = i * orbitals + h * 128
+                    op_wide[h, pl.ds(n * deep + i, m, stride=rows), :] = out[:, low : low + 128]
+
+    def packed(w):
+        first = pl.ds(pl.multiple_of(w * rows, rows), rows)
+        return jnp.concatenate([op_wide[h, first, :] for h in range(halves)], axis=1).astype(bf16)
+
+    def chip_operators(which):
+        left[:slots] = all_fields[pair, which]
+        operators(slots)
+
+        def pack(s, carry):
+            for c in range(cap):
+                op_send[0, which, c, s] = packed(c * blocks + s)
+            return carry
+
+        lax.fori_loop(0, blocks, pack, 0)
+
+    def send_chip_operators(which):
+        def to(s):
+            send(
+                op_send.at[0, which, :, s],
+                op_recv.at[:, me, 0, which],
+                op_sent.at[cap],
+                op_got.at[cap],
+                s,
+            )
+
+        far_then_near(to, to)
+        for c in range(cap):
+            op_recv[c, me, 0, which] = op_send[0, which, c, me]
+
+    def other_operators(c, first, count):
+        for k in range(count):
+            chip = lax.rem(pair + first + k, pairs)
+            for q in range(2):
+                low = (k * 2 + q) * blocks
+                left[low : low + blocks] = all_fields[chip, q, c * blocks : (c + 1) * blocks]
+        operators(count * 2 * blocks)
+
+        def pack(s, carry):
+            for k in range(count):
+                for q in range(2):
+                    op_send[first + k, q, c, s] = packed((k * 2 + q) * blocks + s)
+            return carry
+
+        lax.fori_loop(0, blocks, pack, 0)
+
+        def to(s):
+            send(
+                op_send.at[pl.ds(first, count), :, c, s],
+                op_recv.at[c, me, pl.ds(first, count)],
+                op_sent.at[c],
+                op_got.at[c],
+                s,
+            )
+
+        far_then_near(to, to)
+        for k in range(count):
+            for q in range(2):
+                op_recv[c, me, first + k, q] = op_send[first + k, q, c, me]
+
+    chip_operators(core)
+    pl.semaphore_wait(barrier, blocks - 1)
+
+    partner = pair * 2 + 1 - core
+    beside = (line * 2 + 1 - across) * 2 + core
+
+    def line_at(j):
+        return lax.rem(line + lines - j, lines)
+
+    own = all_fields.at[pair, core]
+    send(own, own, field_send.at[0], field_core.at[0], partner)
+    for j in range(1, lines):
+        peer = (lax.rem(line + j, lines) * 2 + across) * 2 + core
+        send(own, own, field_send.at[2], field_line.at[j], peer)
+    send(own, own, field_send.at[1], field_row.at[0], beside)
+    send_chip_operators(core)
+
+    twin = all_fields.at[pair, 1 - core]
+    wait(twin, field_core.at[0])
+    chip_operators(1 - core)
+    send_chip_operators(1 - core)
+    for j in range(1, lines):
+        held = all_fields.at[line_at(j) * 2 + across, core]
+        wait(held, field_line.at[j])
+        send(held, held, field_send.at[1], field_row.at[j], beside)
+        send(held, held, field_send.at[0], field_core.at[1], partner)
+    for j in range(lines):
+        held = all_fields.at[line_at(j) * 2 + 1 - across, core]
+        wait(held, field_row.at[j])
+        send(held, held, field_send.at[0], field_core.at[1], partner)
+    wait(all_fields.at[pl.ds(0, pairs - 1), 0], field_core.at[1])
+
+    split = pairs // 2
+    for c in range(cap):
+        other_operators(c, 1, split)
+        other_operators(c, 1 + split, pairs - 1 - split)
+
+    rotated_load.wait()
+    strided_relay(rotated_raw, rotated_wide, rotated, 0, nchol)
+    walker_load.wait()
+
+    def taylor(c):
+        group = 4
+
+        @pl.loop(0, blocks // group)
+        def _(g):
+            ops, terms, sums = [], [], []
+            for u in range(group):
+                r = g * group + u
+                chip, q = lax.rem(r, pairs), r // pairs
+                ops.append(
+                    jnp.concatenate(
+                        [
+                            op_recv[c, o, lax.rem(chip + pairs - o // 2, pairs), q]
+                            for o in range(blocks)
+                        ],
+                        axis=0,
+                    )
+                )
+                entry = jnp.maximum(send_walker[(chip * 2 + q) * cap + c], 0)
+                terms.append(walkers[entry])
+                sums.append(terms[u].astype(f32))
+            for degree in range(1, degrees + 1):
+                for u in range(group):
+                    product = lax.dot_general(
+                        terms[u], ops[u], (((1,), (1,)), ((), ())), preferred_element_type=f32
+                    )
+                    terms[u] = (product * (1.0 / degree)).astype(bf16)
+                    sums[u] = sums[u] + terms[u].astype(f32)
+            for u in range(group):
+                r = g * group + u
+                nw_full[c, r] = sums[u].astype(bf16)
+                at = pl.ds(pl.multiple_of(r * electrons, electrons), electrons)
+                for h in range(halves):
+                    totals[h, at, :] = sums[u][:, h * 128 : (h + 1) * 128]
+
+        def turn(o, carry):
+            for e in range(elec):
+                for h in range(halves):
+                    low = e * orbitals + h * 128
+                    nw_send[c, o, :, low : low + 128] = totals[
+                        h, pl.ds(o * elec + e, blocks, stride=electrons), :
+                    ].astype(bf16)
+            return carry
+
+        lax.fori_loop(0, blocks, turn, 0)
+
+        def to_owner(o):
+            send(nw_send.at[c, o], nw_recv.at[c, me], nw_sent.at[c], nw_got.at[c], o)
+
+        far_then_near(to_owner, to_owner)
+        nw_recv[c, me] = nw_send[c, me]
+        mine = pl.ds(pl.multiple_of(side * near, near), near)
+
+        def to_far(d):
+            send(
+                nw_full.at[c, row_of(d), mine],
+                branch.at[c, me, mine],
+                br_sent.at[0],
+                br_got.at[0],
+                d,
+            )
+
+        def to_close(d):
+            send(nw_full.at[c, row_of(d)], branch.at[c, me], br_sent.at[0], br_got.at[0], d)
+
+        far_then_near(to_far, to_close)
+        branch[c, me] = nw_full[c, row_of(me)]
+
+    def bias(c):
+        rows_in = nw_recv[c].reshape(blocks * blocks, elec * orbitals)
+        step = min(256, nchol)
+
+        @pl.loop(0, nchol // step)
+        def _(n):
+            at = pl.ds(pl.multiple_of(n * step, step), step)
+            out = lax.dot_general(
+                rows_in, rotated[at, :], (((1,), (1,)), ((), ())), preferred_element_type=f32
+            ).reshape(blocks, 2, pairs, step)
+            for q in range(2):
+                mine = out[:, q].reshape(blocks * pairs, step)
+                for h in range(step // 128):
+                    part[c, q, n * (step // 128) + h] = mine[:, h * 128 : (h + 1) * 128]
+
+        send(part.at[c, 1 - core], pair_recv.at[c], pair_sent.at[c], pair_got.at[c], partner)
+
+    def reduce(c):
+        wait(pair_recv.at[c], pair_got.at[c])
+
+        def pick(chip, carry):
+            at = pl.ds(chip, blocks, stride=pairs)
+            for h in range(nchol // 128):
+                both = part[c, core, h, at, :] + pair_recv[c, h, at, :]
+                fb_send[c, chip, :, h * 128 : (h + 1) * 128] = both.astype(bf16)
+            return carry
+
+        lax.fori_loop(0, pairs, pick, 0)
+
+        def step(k, carry):
+            chip = lax.rem(pair + pairs // 2 + k, pairs)
+
+            @pl.when(chip != pair)
+            def _():
+                send(
+                    fb_send.at[c, chip],
+                    fb_recv.at[c, pair],
+                    fb_sent.at[c],
+                    fb_got.at[c],
+                    chip * 2 + core,
+                )
+
+            return carry
+
+        lax.fori_loop(0, pairs, step, 0)
+        fb_recv[c, pair] = fb_send[c, pair]
+
+    def finish(c):
+        wait(fb_recv.at[c, pl.ds(0, pairs - 1)], fb_got.at[c])
+        fb_total[c] = lax.fori_loop(
+            1,
+            pairs,
+            lambda s, acc: acc + fb_recv[c, s].astype(f32),
+            fb_recv[c, 0].astype(f32),
+        )
+
+    def forward():
+        count = half * blocks
+        for c in range(cap):
+            block = nw_recv[c, pl.ds(away * half, half)].astype(f32)
+            block = block.reshape(count, elec * orbitals)
+            for h in range(elec * orbitals // 128):
+                fw_wide[h, c * count : (c + 1) * count] = block[:, h * 128 : (h + 1) * 128]
+
+        def gather(t, carry):
+            at = pl.ds(row_of(side * half + t), cap * half, stride=blocks)
+            for h in range(elec * orbitals // 128):
+                fw_send[t, :, h * 128 : (h + 1) * 128] = fw_wide[h, at, :].astype(bf16)
+            return carry
+
+        lax.fori_loop(0, half, gather, 0)
+
+        def step(k, carry):
+            t = lax.rem(local + k, half)
+            send(fw_send.at[t], fw_recv.at[local], fw_sent.at[0], fw_got.at[0], side * half + t)
+            return carry
+
+        lax.fori_loop(1, half, step, 0)
+        fw_recv[local] = fw_send[local]
+
+    def collect():
+        wait(fw_recv.at[pl.ds(0, half - 1)], fw_got.at[0])
+
+        def fold(o, carry):
+            block = fw_recv[o].astype(f32)
+            for e in range(elec):
+                for h in range(halves):
+                    low = e * orbitals + h * 128
+                    fw_rows[h, pl.ds(o * elec + e, cap * half, stride=near), :] = block[
+                        :, low : low + 128
+                    ]
+            return carry
+
+        lax.fori_loop(0, half, fold, 0)
+        wait(branch.at[:, pl.ds(0, half - 1 + half // 2)], br_got.at[0])
+
+        def put(s, carry):
+            for c in range(cap):
+                at = pl.ds(pl.multiple_of((c * half + s) * near, near), near)
+                value = jnp.concatenate([fw_rows[h, at, :] for h in range(halves)], axis=1)
+                mine = pl.ds(pl.multiple_of(side * near, near), near)
+                branch[c, away * half + s, mine] = value.astype(bf16)
+            return carry
+
+        lax.fori_loop(0, half, put, 0)
+
+        def walker_out(p, carry):
+            entry = slot_row[p]
+            new_walkers[p] = branch[lax.rem(entry, cap), entry // cap]
+            return carry
+
+        lax.fori_loop(0, slots, walker_out, 0)
+
+    wait(op_recv.at[:, pl.ds(0, blocks - 1), 0], op_got.at[cap])
+    for c in range(cap):
+        wait(op_recv.at[c, pl.ds(0, blocks - 1), pl.ds(1, pairs - 1)], op_got.at[c])
+        taylor(c)
+    for c in range(cap):
+        wait(nw_recv.at[c, pl.ds(0, blocks - 1)], nw_got.at[c])
+        bias(c)
+        if c == cap - 1:
+            forward()
+        reduce(c)
+    collect()
+    for c in range(cap):
+        finish(c)
+
+    def bias_out(p, carry):
+        entry = slot_row[p]
+        force_bias[pl.ds(p, 1), :] = fb_total[lax.rem(entry, cap), pl.ds(entry // cap, 1), :]
+        return carry
+
+    lax.fori_loop(0, slots, bias_out, 0)
+
+    wait(all_fields.at[:, 0], field_send.at[0])
+    wait(all_fields.at[pl.ds(0, lines), 0], field_send.at[1])
+    wait(all_fields.at[pl.ds(0, lines - 1), 0], field_send.at[2])
+    wait(op_recv.at[:, pl.ds(0, blocks - 1), 0], op_sent.at[cap])
+    wait(branch.at[:, pl.ds(0, half - 1 + half // 2)], br_sent.at[0])
+    wait(fw_send.at[pl.ds(0, half - 1)], fw_sent.at[0])
+    for c in range(cap):
+        wait(op_recv.at[c, pl.ds(0, blocks - 1), pl.ds(1, pairs - 1)], op_sent.at[c])
+        wait(nw_send.at[c, pl.ds(0, blocks - 1)], nw_sent.at[c])
+        wait(pair_recv.at[c], pair_sent.at[c])
+        wait(fb_send.at[c, pl.ds(0, pairs - 1)], fb_sent.at[c])
+
+
+def parent_shards(blocks, walkers, fields, chol_vectors, rotated, send_walker, slot_row):
+    slots, electrons, orbitals = walkers.shape
+    nchol, rows, _ = chol_vectors.shape
+    elec = rotated.shape[1]
+    cap = send_walker.shape[-1]
+    bf16, f32 = jnp.bfloat16, jnp.float32
+    pairs, lines, half = blocks // 2, blocks // 4, blocks // 2
+    halves, near = orbitals // 128, electrons // 2
+    most = max(pairs // 2 * 2 * blocks, slots)
+    wide = elec * orbitals
+    vmem, smem, anywhere = (
+        pl.BlockSpec(memory_space=m) for m in (pltpu.VMEM, pltpu.SMEM, pl.ANY)
+    )
+    dma = pltpu.SemaphoreType.DMA
+    return pl.pallas_call(
+        functools.partial(parent_kernel, (blocks, cap, rows, elec)),
+        out_shape=(
+            jax.ShapeDtypeStruct(walkers.shape, bf16),
+            jax.ShapeDtypeStruct((slots, nchol), f32),
+        ),
+        in_specs=[smem, smem, vmem, anywhere, anywhere, anywhere],
+        out_specs=(vmem, vmem),
+        scratch_shapes=[
+            pltpu.VMEM(walkers.shape, bf16),
+            pltpu.VMEM(chol_vectors.shape, bf16),
+            pltpu.VMEM((halves, rows * unfold_depth, 128), f32),
+            pltpu.VMEM((nchol, rows * orbitals), bf16),
+            pltpu.VMEM(rotated.shape, bf16),
+            pltpu.VMEM((halves, elec * unfold_depth, 128), f32),
+            pltpu.VMEM((nchol, wide), bf16),
+            pltpu.VMEM((pairs, 2, slots, nchol), bf16),
+            pltpu.VMEM((most, nchol), bf16),
+            pltpu.VMEM((halves, most * rows, 128), f32),
+            pltpu.VMEM((pairs, 2, cap, blocks, rows, orbitals), bf16),
+            pltpu.VMEM((cap, blocks, pairs, 2, rows, orbitals), bf16),
+            pltpu.VMEM((halves, blocks * electrons, 128), f32),
+            pltpu.VMEM((cap, blocks, electrons, orbitals), bf16),
+            pltpu.VMEM((cap, blocks, blocks, wide), bf16),
+            pltpu.VMEM((cap, blocks, blocks, wide), bf16),
+            pltpu.VMEM((cap, 2, nchol // 128, blocks * pairs, 128), f32),
+            pltpu.VMEM((cap, nchol // 128, blocks * pairs, 128), f32),
+            pltpu.VMEM((cap, pairs, blocks, nchol), bf16),
+            pltpu.VMEM((cap, pairs, blocks, nchol), bf16),
+            pltpu.VMEM((cap, blocks, nchol), f32),
+            pltpu.VMEM((wide // 128, cap * half * blocks, 128), f32),
+            pltpu.VMEM((half, cap * half, wide), bf16),
+            pltpu.VMEM((half, cap * half, wide), bf16),
+            pltpu.VMEM((halves, cap * half * near, 128), f32),
+            pltpu.VMEM((cap, blocks, electrons, orbitals), bf16),
+            dma((6,)),
+            dma((3,)),
+            dma((2,)),
+            dma((lines,)),
+            dma((lines,)),
+            dma((cap + 1,)),
+            dma((cap + 1,)),
+            dma((cap,)),
+            dma((cap,)),
+            dma((1,)),
+            dma((1,)),
+            dma((cap,)),
+            dma((cap,)),
+            dma((cap,)),
+            dma((cap,)),
+            dma((1,)),
+            dma((1,)),
+        ],
+        compiler_params=pltpu.CompilerParams(
+            collective_id=1, has_side_effects=True, vmem_limit_bytes=60 * 1024 * 1024
+        ),
+    )(send_walker.reshape(-1), slot_row, fields, walkers, chol_vectors, rotated)
+
+
+def plan(blocks, walkers, fields, chol_vectors, rotated, send_walker, slot_row):
+    every_entry = blocks * send_walker.shape[-1] == walkers.shape[0]
+    step = parent_shards if every_entry and blocks % 8 == 0 else shards
+    return step(blocks, walkers, fields, chol_vectors, rotated, send_walker, slot_row)
+
+
 def solution(mesh):
     in_specs = (
         P(("grp", "chol"), None, None),
@@ -396,7 +960,7 @@
     )
     out_specs = (P(("grp", "chol"), None, None), P(("grp", "chol"), None))
     return jax.shard_map(
-        functools.partial(shards, mesh.shape["chol"]),
+        functools.partial(plan, mesh.shape["chol"]),
         mesh=mesh,
         in_specs=in_specs,
         out_specs=out_specs,

time: 174 us -> 169 us (0.971)
  Pallas kernels: 168 us -> 163 us
    pallas_call x1, Pallas kernels: 168 us -> 163 us  [parent_shards(): pl.pallas_call(functools.partial(parent_kernel, (blocks, cap, rows, elec)...]
where the time goes in v1:
time: 169 us
  Pallas kernels  163 us (96%)
  local copies, waits for them, and re-layouts  5.23 us (3%)
    pallas_call x1, Pallas kernels, parent_shards(): pl.pallas_call(functools.partial(parent_kernel, (blocks, cap, rows, elec)...  163 us
    unnamed x3, local copies, waits for them, and re-layouts  4.63 us

profile of v1, /device:TPU:0, one launch (start us, length us, event | category | flops | bytes accessed | tf_op | source)
XLA Modules:
  0.0 169.2 jit_solution(9980415764152277796)
XLA Ops:
  0.6 0.8 copy.9
  1.4 0.6 reshape.7.send_walker
  2.0 163.3 %shard_map.77 = (bf16[32,64,256]{2,1,0:T(8,128)(2,1)}, f32[32,1024]{1,0:T(8,128)}) custom-call(s32[32]{0:T(128)} %reshape.7.send_walker, s32[32]{0:T(128)} %slot_row.1, bf16[32,1024]{1,0:T(8,128)(2,1)} %fields.1, bf16[32,64,256]{2,1,0:T(8,128)(2,1)} %walkers_hbm.1, bf16[1024,16,256]{2,1,0:T(8,128)(2,1)} %chol_hbm.1, bf16[1024,4,256]{2,1,0:T(4,128)(2,1)} %rotated_hbm.1), custom_call_target="tpu_custom_call" | custom-call | tf_op jit(solution)/shard_map/pallas_call | solution.py:887
  165.3 2.3 %copy.12 = bf16[32,64,256]{2,1,0:T(8,128)(2,1)} copy(bf16[32,64,256]{2,1,0:T(8,128)(2,1)} %get-tuple-element.4) | data formatting | bytes 2097152
  167.6 1.6 copy.13

commit v2 on v1

--- a/solution.py
+++ b/solution.py
@@ -433,6 +433,8 @@
     nw_recv,
     part,
     pair_recv,
+    row_send,
+    row_recv,
     fb_send,
     fb_recv,
     fb_total,
@@ -454,6 +456,8 @@
     br_got,
     pair_sent,
     pair_got,
+    row_sent,
+    row_got,
     fb_sent,
     fb_got,
     fw_sent,
@@ -565,7 +569,7 @@
 
         def pack(s, carry):
             for c in range(cap):
-                op_send[0, which, c, s] = packed(c * blocks + s)
+                op_send[c, s, 0, which] = packed(c * blocks + s)
             return carry
 
         lax.fori_loop(0, blocks, pack, 0)
@@ -573,7 +577,7 @@
     def send_chip_operators(which):
         def to(s):
             send(
-                op_send.at[0, which, :, s],
+                op_send.at[:, s, 0, which],
                 op_recv.at[:, me, 0, which],
                 op_sent.at[cap],
                 op_got.at[cap],
@@ -582,27 +586,28 @@
 
         far_then_near(to, to)
         for c in range(cap):
-            op_recv[c, me, 0, which] = op_send[0, which, c, me]
+            op_recv[c, me, 0, which] = op_send[c, me, 0, which]
 
     def other_operators(c, first, count):
         for k in range(count):
             chip = lax.rem(pair + first + k, pairs)
             for q in range(2):
                 low = (k * 2 + q) * blocks
-                left[low : low + blocks] = all_fields[chip, q, c * blocks : (c + 1) * blocks]
+                at = pl.ds(pl.multiple_of(c * blocks, blocks), blocks)
+                left[low : low + blocks] = all_fields[chip, q, at]
         operators(count * 2 * blocks)
 
         def pack(s, carry):
             for k in range(count):
                 for q in range(2):
-                    op_send[first + k, q, c, s] = packed((k * 2 + q) * blocks + s)
+                    op_send[c, s, first + k, q] = packed((k * 2 + q) * blocks + s)
             return carry
 
         lax.fori_loop(0, blocks, pack, 0)
 
         def to(s):
             send(
-                op_send.at[pl.ds(first, count), :, c, s],
+                op_send.at[c, s, pl.ds(first, count)],
                 op_recv.at[c, me, pl.ds(first, count)],
                 op_sent.at[c],
                 op_got.at[c],
@@ -612,10 +617,7 @@
         far_then_near(to, to)
         for k in range(count):
             for q in range(2):
-                op_recv[c, me, first + k, q] = op_send[first + k, q, c, me]
-
-    chip_operators(core)
-    pl.semaphore_wait(barrier, blocks - 1)
+                op_recv[c, me, first + k, q] = op_send[c, me, first + k, q]
 
     partner = pair * 2 + 1 - core
     beside = (line * 2 + 1 - across) * 2 + core
@@ -623,23 +625,29 @@
     def line_at(j):
         return lax.rem(line + lines - j, lines)
 
-    own = all_fields.at[pair, core]
+    own, twin = all_fields.at[pair, core], all_fields.at[pair, 1 - core]
+    pl.semaphore_wait(barrier, blocks - 1)
     send(own, own, field_send.at[0], field_core.at[0], partner)
     for j in range(1, lines):
         peer = (lax.rem(line + j, lines) * 2 + across) * 2 + core
         send(own, own, field_send.at[2], field_line.at[j], peer)
     send(own, own, field_send.at[1], field_row.at[0], beside)
-    send_chip_operators(core)
-
-    twin = all_fields.at[pair, 1 - core]
-    wait(twin, field_core.at[0])
-    chip_operators(1 - core)
-    send_chip_operators(1 - core)
-    for j in range(1, lines):
-        held = all_fields.at[line_at(j) * 2 + across, core]
-        wait(held, field_line.at[j])
-        send(held, held, field_send.at[1], field_row.at[j], beside)
-        send(held, held, field_send.at[0], field_core.at[1], partner)
+
+    @pl.loop(0, 2)
+    def _(t):
+        @pl.when(t == 1)
+        def _():
+            for j in range(1, lines):
+                held = all_fields.at[line_at(j) * 2 + across, core]
+                wait(held, field_line.at[j])
+                send(held, held, field_send.at[1], field_row.at[j], beside)
+                send(held, held, field_send.at[0], field_core.at[1], partner)
+            wait(twin, field_core.at[0])
+
+        which = lax.rem(core + t, 2)
+        chip_operators(which)
+        send_chip_operators(which)
+
     for j in range(lines):
         held = all_fields.at[line_at(j) * 2 + 1 - across, core]
         wait(held, field_row.at[j])
@@ -647,7 +655,9 @@
     wait(all_fields.at[pl.ds(0, pairs - 1), 0], field_core.at[1])
 
     split = pairs // 2
-    for c in range(cap):
+
+    @pl.loop(0, cap)
+    def _(c):
         other_operators(c, 1, split)
         other_operators(c, 1 + split, pairs - 1 - split)
 
@@ -740,41 +750,54 @@
 
         send(part.at[c, 1 - core], pair_recv.at[c], pair_sent.at[c], pair_got.at[c], partner)
 
+    def reduced(c, chip, h):
+        at = pl.ds(chip, blocks, stride=pairs)
+        return part[c, core, h, at, :] + pair_recv[c, h, at, :]
+
     def reduce(c):
         wait(pair_recv.at[c], pair_got.at[c])
 
-        def pick(chip, carry):
-            at = pl.ds(chip, blocks, stride=pairs)
+        def pick(z, carry):
             for h in range(nchol // 128):
-                both = part[c, core, h, at, :] + pair_recv[c, h, at, :]
-                fb_send[c, chip, :, h * 128 : (h + 1) * 128] = both.astype(bf16)
-            return carry
-
-        lax.fori_loop(0, pairs, pick, 0)
+                both = reduced(c, z * 2 + 1 - across, h)
+                row_send[c, z, :, h * 128 : (h + 1) * 128] = both.astype(bf16)
+            return carry
+
+        lax.fori_loop(0, lines, pick, 0)
+        send(row_send.at[c], row_recv.at[c], row_sent.at[c], row_got.at[c], beside)
+
+    def spread(c):
+        wait(row_recv.at[c], row_got.at[c])
+
+        def pick(z, carry):
+            for h in range(nchol // 128):
+                low = h * 128
+                both = reduced(c, z * 2 + across, h)
+                both = both + row_recv[c, z, :, low : low + 128].astype(f32)
+                fb_send[c, z, :, low : low + 128] = both.astype(bf16)
+            return carry
+
+        lax.fori_loop(0, lines, pick, 0)
 
         def step(k, carry):
-            chip = lax.rem(pair + pairs // 2 + k, pairs)
-
-            @pl.when(chip != pair)
-            def _():
-                send(
-                    fb_send.at[c, chip],
-                    fb_recv.at[c, pair],
-                    fb_sent.at[c],
-                    fb_got.at[c],
-                    chip * 2 + core,
-                )
-
-            return carry
-
-        lax.fori_loop(0, pairs, step, 0)
-        fb_recv[c, pair] = fb_send[c, pair]
+            z = lax.rem(line + k, lines)
+            send(
+                fb_send.at[c, z],
+                fb_recv.at[c, line],
+                fb_sent.at[c],
+                fb_got.at[c],
+                (z * 2 + across) * 2 + core,
+            )
+            return carry
+
+        lax.fori_loop(1, lines, step, 0)
+        fb_recv[c, line] = fb_send[c, line]
 
     def finish(c):
-        wait(fb_recv.at[c, pl.ds(0, pairs - 1)], fb_got.at[c])
+        wait(fb_recv.at[c, pl.ds(0, lines - 1)], fb_got.at[c])
         fb_total[c] = lax.fori_loop(
             1,
-            pairs,
+            lines,
             lambda s, acc: acc + fb_recv[c, s].astype(f32),
             fb_recv[c, 0].astype(f32),
         )
@@ -846,6 +869,7 @@
         if c == cap - 1:
             forward()
         reduce(c)
+        spread(c)
     collect()
     for c in range(cap):
         finish(c)
@@ -867,7 +891,8 @@
         wait(op_recv.at[c, pl.ds(0, blocks - 1), pl.ds(1, pairs - 1)], op_sent.at[c])
         wait(nw_send.at[c, pl.ds(0, blocks - 1)], nw_sent.at[c])
         wait(pair_recv.at[c], pair_sent.at[c])
-        wait(fb_send.at[c, pl.ds(0, pairs - 1)], fb_sent.at[c])
+        wait(row_send.at[c], row_sent.at[c])
+        wait(fb_send.at[c, pl.ds(0, lines - 1)], fb_sent.at[c])
 
 
 def parent_shards(blocks, walkers, fields, chol_vectors, rotated, send_walker, slot_row):
@@ -903,7 +928,7 @@
             pltpu.VMEM((pairs, 2, slots, nchol), bf16),
             pltpu.VMEM((most, nchol), bf16),
             pltpu.VMEM((halves, most * rows, 128), f32),
-            pltpu.VMEM((pairs, 2, cap, blocks, rows, orbitals), bf16),
+            pltpu.VMEM((cap, blocks, pairs, 2, rows, orbitals), bf16),
             pltpu.VMEM((cap, blocks, pairs, 2, rows, orbitals), bf16),
             pltpu.VMEM((halves, blocks * electrons, 128), f32),
             pltpu.VMEM((cap, blocks, electrons, orbitals), bf16),
@@ -911,8 +936,10 @@
             pltpu.VMEM((cap, blocks, blocks, wide), bf16),
             pltpu.VMEM((cap, 2, nchol // 128, blocks * pairs, 128), f32),
             pltpu.VMEM((cap, nchol // 128, blocks * pairs, 128), f32),
-            pltpu.VMEM((cap, pairs, blocks, nchol), bf16),
-            pltpu.VMEM((cap, pairs, blocks, nchol), bf16),
+            pltpu.VMEM((cap, lines, blocks, nchol), bf16),
+            pltpu.VMEM((cap, lines, blocks, nchol), bf16),
+            pltpu.VMEM((cap, lines, blocks, nchol), bf16),
+            pltpu.VMEM((cap, lines, blocks, nchol), bf16),
             pltpu.VMEM((cap, blocks, nchol), f32),
             pltpu.VMEM((wide // 128, cap * half * blocks, 128), f32),
             pltpu.VMEM((half, cap * half, wide), bf16),
@@ -934,6 +961,8 @@
             dma((cap,)),
             dma((cap,)),
             dma((cap,)),
+            dma((cap,)),
+            dma((cap,)),
             dma((1,)),
             dma((1,)),
         ],

time: 169 us -> 165 us (0.976)
  Pallas kernels: 163 us -> 159 us
    pallas_call x1, Pallas kernels: 163 us -> 159 us  [parent_shards(): pl.pallas_call(functools.partial(parent_kernel, (blocks, cap, rows, elec)...]
where the time goes in v2:
time: 165 us
  Pallas kernels  159 us (96%)
  local copies, waits for them, and re-layouts  5.23 us (3%)
    pallas_call x1, Pallas kernels, parent_shards(): pl.pallas_call(functools.partial(parent_kernel, (blocks, cap, rows, elec)...  159 us
    unnamed x3, local copies, waits for them, and re-layouts  4.63 us

profile of v2, /device:TPU:0, one launch (start us, length us, event | category | flops | bytes accessed | tf_op | source)
XLA Modules:
  0.0 164.7 jit_solution(8843066385819247832)
XLA Ops:
  0.6 0.8 copy.9
  1.4 0.6 reshape.7.send_walker
  2.0 158.8 %shard_map.77 = (bf16[32,64,256]{2,1,0:T(8,128)(2,1)}, f32[32,1024]{1,0:T(8,128)}) custom-call(s32[32]{0:T(128)} %reshape.7.send_walker, s32[32]{0:T(128)} %slot_row.1, bf16[32,1024]{1,0:T(8,128)(2,1)} %fields.1, bf16[32,64,256]{2,1,0:T(8,128)(2,1)} %walkers_hbm.1, bf16[1024,16,256]{2,1,0:T(8,128)(2,1)} %chol_hbm.1, bf16[1024,4,256]{2,1,0:T(4,128)(2,1)} %rotated_hbm.1), custom_call_target="tpu_custom_call" | custom-call | tf_op jit(solution)/shard_map/pallas_call | solution.py:912
  160.8 2.3 %copy.12 = bf16[32,64,256]{2,1,0:T(8,128)(2,1)} copy(bf16[32,64,256]{2,1,0:T(8,128)(2,1)} %get-tuple-element.4) | data formatting | bytes 2097152
  163.1 1.6 copy.13

commit v3 on v2

--- a/solution.py
+++ b/solution.py
@@ -385,21 +385,15 @@
     )
 
 
-def strided_relay(source, scratch, target, start, count):
+def turned(source, target, start, count):
     rows, orbitals = source.shape[1:]
-    step = min(scratch.shape[1] // rows, count)
+    step = 16
 
     def body(b, carry):
         first = pl.multiple_of(start + b * step, step)
-        block = source[pl.ds(first, step)].astype(jnp.float32).reshape(step * rows, orbitals)
-        for h in range(orbitals // 128):
-            scratch[h, : step * rows] = block[:, h * 128 : (h + 1) * 128]
+        block = jnp.swapaxes(source[pl.ds(first, step)], 0, 1)
         for r in range(rows):
-            for h in range(orbitals // 128):
-                low = r * orbitals + h * 128
-                target[pl.ds(first, step), low : low + 128] = scratch[
-                    h, pl.ds(r, step, stride=rows), :
-                ].astype(jnp.bfloat16)
+            target[pl.ds(first, step), r * orbitals : (r + 1) * orbitals] = block[r]
         return carry
 
     lax.fori_loop(0, count // step, body, 0)
@@ -417,17 +411,14 @@
     force_bias,
     walkers,
     chol_raw,
-    chol_wide,
     chol,
     rotated_raw,
-    rotated_wide,
     rotated,
     all_fields,
     left,
-    op_wide,
+    op_rows,
     op_send,
     op_recv,
-    totals,
     nw_full,
     nw_send,
     nw_recv,
@@ -469,6 +460,7 @@
     halves = orbitals // 128
     me = lax.axis_index("chol")
     pairs, lines, half = blocks // 2, blocks // 4, blocks // 2
+    hop = stride_of(blocks)
     core, pair = lax.rem(me, 2), me // 2
     line, across = pair // 2, lax.rem(pair, 2)
     side, local = me // half, lax.rem(me, half)
@@ -488,6 +480,13 @@
             device_id={"chol": peer},
             device_id_type=MESH,
         ).start()
+
+    def everyone(to):
+        def step(t, carry):
+            to(lax.rem(me + t * hop, blocks))
+            return carry
+
+        lax.fori_loop(1, blocks, step, 0)
 
     def far_then_near(far, close):
         def first(t, carry):
@@ -542,11 +541,11 @@
 
     for p in range(pieces):
         chol_loads[p].wait()
-        strided_relay(chol_raw, chol_wide, chol, p * span, span)
+        turned(chol_raw, chol, p * span, span)
 
     scale = field_scale / math.sqrt(nchol)
     cols = rows * orbitals
-    tile = min(512, cols)
+    tile = min(1024, cols)
     deep = tile // orbitals
 
     def operators(m):
@@ -555,24 +554,16 @@
             at = pl.ds(pl.multiple_of(n * tile, tile), tile)
             out = jnp.dot(left[:m], chol[:, at], preferred_element_type=f32) * scale
             for i in range(deep):
-                for h in range(halves):
-                    low = i * orbitals + h * 128
-                    op_wide[h, pl.ds(n * deep + i, m, stride=rows), :] = out[:, low : low + 128]
-
-    def packed(w):
-        first = pl.ds(pl.multiple_of(w * rows, rows), rows)
-        return jnp.concatenate([op_wide[h, first, :] for h in range(halves)], axis=1).astype(bf16)
+                op_rows[n * deep + i, :m] = out[:, i * orbitals : (i + 1) * orbitals].astype(bf16)
+
+    def packed(b):
+        return jnp.swapaxes(op_rows[:, b * blocks : (b + 1) * blocks], 0, 1)
 
     def chip_operators(which):
         left[:slots] = all_fields[pair, which]
         operators(slots)
-
-        def pack(s, carry):
-            for c in range(cap):
-                op_send[c, s, 0, which] = packed(c * blocks + s)
-            return carry
-
-        lax.fori_loop(0, blocks, pack, 0)
+        for c in range(cap):
+            op_send[c, :, 0, which] = packed(c)
 
     def send_chip_operators(which):
         def to(s):
@@ -584,7 +575,7 @@
                 s,
             )
 
-        far_then_near(to, to)
+        everyone(to)
         for c in range(cap):
             op_recv[c, me, 0, which] = op_send[c, me, 0, which]
 
@@ -597,13 +588,9 @@
                 left[low : low + blocks] = all_fields[chip, q, at]
         operators(count * 2 * blocks)
 
-        def pack(s, carry):
-            for k in range(count):
-                for q in range(2):
-                    op_send[c, s, first + k, q] = packed((k * 2 + q) * blocks + s)
-            return carry
-
-        lax.fori_loop(0, blocks, pack, 0)
+        for k in range(count):
+            for q in range(2):
+                op_send[c, :, first + k, q] = packed(k * 2 + q)
 
         def to(s):
             send(
@@ -614,7 +601,7 @@
                 s,
             )
 
-        far_then_near(to, to)
+        everyone(to)
         for k in range(count):
             for q in range(2):
                 op_recv[c, me, first + k, q] = op_send[c, me, first + k, q]
@@ -662,7 +649,7 @@
         other_operators(c, 1 + split, pairs - 1 - split)
 
     rotated_load.wait()
-    strided_relay(rotated_raw, rotated_wide, rotated, 0, nchol)
+    turned(rotated_raw, rotated, 0, nchol)
     walker_load.wait()
 
     def taylor(c):
@@ -696,25 +683,17 @@
             for u in range(group):
                 r = g * group + u
                 nw_full[c, r] = sums[u].astype(bf16)
-                at = pl.ds(pl.multiple_of(r * electrons, electrons), electrons)
-                for h in range(halves):
-                    totals[h, at, :] = sums[u][:, h * 128 : (h + 1) * 128]
-
-        def turn(o, carry):
-            for e in range(elec):
-                for h in range(halves):
-                    low = e * orbitals + h * 128
-                    nw_send[c, o, :, low : low + 128] = totals[
-                        h, pl.ds(o * elec + e, blocks, stride=electrons), :
-                    ].astype(bf16)
-            return carry
-
-        lax.fori_loop(0, blocks, turn, 0)
+
+        for o in range(0, blocks, 16 // elec):
+            block = jnp.swapaxes(nw_full[c, :, o * elec : o * elec + 16], 0, 1)
+            for e in range(16):
+                low = e % elec * orbitals
+                nw_send[c, o + e // elec, :, low : low + orbitals] = block[e]
 
         def to_owner(o):
             send(nw_send.at[c, o], nw_recv.at[c, me], nw_sent.at[c], nw_got.at[c], o)
 
-        far_then_near(to_owner, to_owner)
+        everyone(to_owner)
         nw_recv[c, me] = nw_send[c, me]
         mine = pl.ds(pl.multiple_of(side * near, near), near)
 
@@ -920,17 +899,14 @@
         scratch_shapes=[
             pltpu.VMEM(walkers.shape, bf16),
             pltpu.VMEM(chol_vectors.shape, bf16),
-            pltpu.VMEM((halves, rows * unfold_depth, 128), f32),
             pltpu.VMEM((nchol, rows * orbitals), bf16),
             pltpu.VMEM(rotated.shape, bf16),
-            pltpu.VMEM((halves, elec * unfold_depth, 128), f32),
             pltpu.VMEM((nchol, wide), bf16),
             pltpu.VMEM((pairs, 2, slots, nchol), bf16),
             pltpu.VMEM((most, nchol), bf16),
-            pltpu.VMEM((halves, most * rows, 128), f32),
+            pltpu.VMEM((rows, most, orbitals), bf16),
             pltpu.VMEM((cap, blocks, pairs, 2, rows, orbitals), bf16),
             pltpu.VMEM((cap, blocks, pairs, 2, rows, orbitals), bf16),
-            pltpu.VMEM((halves, blocks * electrons, 128), f32),
             pltpu.VMEM((cap, blocks, electrons, orbitals), bf16),
             pltpu.VMEM((cap, blocks, blocks, wide), bf16),
             pltpu.VMEM((cap, blocks, blocks, wide), bf16),

time: 165 us -> 159 us (0.964)
  Pallas kernels: 159 us -> 153 us
    pallas_call x1, Pallas kernels: 159 us -> 153 us  [parent_shards(): pl.pallas_call(functools.partial(parent_kernel, (blocks, cap, rows, elec)...]
where the time goes in v3:
time: 159 us
  Pallas kernels  153 us (96%)
  local copies, waits for them, and re-layouts  5.23 us (3%)
    pallas_call x1, Pallas kernels, parent_shards(): pl.pallas_call(functools.partial(parent_kernel, (blocks, cap, rows, elec)...  153 us
    unnamed x3, local copies, waits for them, and re-layouts  4.63 us

profile of v3, /device:TPU:0, one launch (start us, length us, event | category | flops | bytes accessed | tf_op | source)
XLA Modules:
  0.0 158.6 jit_solution(11010967862883725249)
XLA Ops:
  0.6 0.8 copy.9
  1.4 0.6 reshape.7.send_walker
  2.0 152.7 %shard_map.77 = (bf16[32,64,256]{2,1,0:T(8,128)(2,1)}, f32[32,1024]{1,0:T(8,128)}) custom-call(s32[32]{0:T(128)} %reshape.7.send_walker, s32[32]{0:T(128)} %slot_row.1, bf16[32,1024]{1,0:T(8,128)(2,1)} %fields.1, bf16[32,64,256]{2,1,0:T(8,128)(2,1)} %walkers_hbm.1, bf16[1024,16,256]{2,1,0:T(8,128)(2,1)} %chol_hbm.1, bf16[1024,4,256]{2,1,0:T(4,128)(2,1)} %rotated_hbm.1), custom_call_target="tpu_custom_call" | custom-call | tf_op jit(solution)/shard_map/pallas_call | solution.py:891
  154.7 2.3 %copy.12 = bf16[32,64,256]{2,1,0:T(8,128)(2,1)} copy(bf16[32,64,256]{2,1,0:T(8,128)(2,1)} %get-tuple-element.4) | data formatting | bytes 2097152
  157.0 1.6 copy.13

commit v4 on v3

--- a/solution.py
+++ b/solution.py
@@ -407,8 +407,8 @@
     walkers_hbm,
     chol_hbm,
     rotated_hbm,
-    new_walkers,
-    force_bias,
+    branch,
+    fb_total,
     walkers,
     chol_raw,
     chol,
@@ -428,12 +428,10 @@
     row_recv,
     fb_send,
     fb_recv,
-    fb_total,
     fw_wide,
     fw_send,
     fw_recv,
     fw_rows,
-    branch,
     load_sems,
     field_send,
     field_core,
@@ -488,18 +486,6 @@
 
         lax.fori_loop(1, blocks, step, 0)
 
-    def far_then_near(far, close):
-        def first(t, carry):
-            far(away * half + lax.rem(local + t, half))
-            return carry
-
-        def second(t, carry):
-            close(side * half + lax.rem(local + t, half))
-            return carry
-
-        lax.fori_loop(0, half, first, 0)
-        lax.fori_loop(1, half, second, 0)
-
     def row_of(d):
         return lax.rem(d, 2) * pairs + d // 2
 
@@ -670,7 +656,7 @@
                         axis=0,
                     )
                 )
-                entry = jnp.maximum(send_walker[(chip * 2 + q) * cap + c], 0)
+                entry = jnp.maximum(send_walker[c, chip * 2 + q], 0)
                 terms.append(walkers[entry])
                 sums.append(terms[u].astype(f32))
             for degree in range(1, degrees + 1):
@@ -697,19 +683,22 @@
         nw_recv[c, me] = nw_send[c, me]
         mine = pl.ds(pl.multiple_of(side * near, near), near)
 
-        def to_far(d):
-            send(
-                nw_full.at[c, row_of(d), mine],
-                branch.at[c, me, mine],
-                br_sent.at[0],
-                br_got.at[0],
-                d,
-            )
-
-        def to_close(d):
-            send(nw_full.at[c, row_of(d)], branch.at[c, me], br_sent.at[0], br_got.at[0], d)
-
-        far_then_near(to_far, to_close)
+        def to_slot(d):
+            @pl.when(d // half != side)
+            def _():
+                send(
+                    nw_full.at[c, row_of(d), mine],
+                    branch.at[c, me, mine],
+                    br_sent.at[0],
+                    br_got.at[0],
+                    d,
+                )
+
+            @pl.when(d // half == side)
+            def _():
+                send(nw_full.at[c, row_of(d)], branch.at[c, me], br_sent.at[0], br_got.at[0], d)
+
+        everyone(to_slot)
         branch[c, me] = nw_full[c, row_of(me)]
 
     def bias(c):
@@ -830,13 +819,6 @@
             return carry
 
         lax.fori_loop(0, half, put, 0)
-
-        def walker_out(p, carry):
-            entry = slot_row[p]
-            new_walkers[p] = branch[lax.rem(entry, cap), entry // cap]
-            return carry
-
-        lax.fori_loop(0, slots, walker_out, 0)
 
     wait(op_recv.at[:, pl.ds(0, blocks - 1), 0], op_got.at[cap])
     for c in range(cap):
@@ -853,13 +835,6 @@
     for c in range(cap):
         finish(c)
 
-    def bias_out(p, carry):
-        entry = slot_row[p]
-        force_bias[pl.ds(p, 1), :] = fb_total[lax.rem(entry, cap), pl.ds(entry // cap, 1), :]
-        return carry
-
-    lax.fori_loop(0, slots, bias_out, 0)
-
     wait(all_fields.at[:, 0], field_send.at[0])
     wait(all_fields.at[pl.ds(0, lines), 0], field_send.at[1])
     wait(all_fields.at[pl.ds(0, lines - 1), 0], field_send.at[2])
@@ -872,6 +847,17 @@
         wait(pair_recv.at[c], pair_sent.at[c])
         wait(row_send.at[c], row_sent.at[c])
         wait(fb_send.at[c, pl.ds(0, lines - 1)], fb_sent.at[c])
+
+
+def place_kernel(slot_row, branch, fb_total, new_walkers, force_bias):
+    cap = branch.shape[0]
+
+    @pl.loop(0, slot_row.shape[0])
+    def _(p):
+        entry = slot_row[p]
+        c, s = lax.rem(entry, cap), entry // cap
+        new_walkers[p] = branch[c, s]
+        force_bias[pl.ds(p, 1), :] = fb_total[c, pl.ds(s, 1), :]
 
 
 def parent_shards(blocks, walkers, fields, chol_vectors, rotated, send_walker, slot_row):
@@ -888,11 +874,11 @@
         pl.BlockSpec(memory_space=m) for m in (pltpu.VMEM, pltpu.SMEM, pl.ANY)
     )
     dma = pltpu.SemaphoreType.DMA
-    return pl.pallas_call(
+    branch, fb_total = pl.pallas_call(
         functools.partial(parent_kernel, (blocks, cap, rows, elec)),
         out_shape=(
-            jax.ShapeDtypeStruct(walkers.shape, bf16),
-            jax.ShapeDtypeStruct((slots, nchol), f32),
+            jax.ShapeDtypeStruct((cap, blocks, electrons, orbitals), bf16),
+            jax.ShapeDtypeStruct((cap, blocks, nchol), f32),
         ),
         in_specs=[smem, smem, vmem, anywhere, anywhere, anywhere],
         out_specs=(vmem, vmem),
@@ -916,12 +902,10 @@
             pltpu.VMEM((cap, lines, blocks, nchol), bf16),
             pltpu.VMEM((cap, lines, blocks, nchol), bf16),
             pltpu.VMEM((cap, lines, blocks, nchol), bf16),
-            pltpu.VMEM((cap, blocks, nchol), f32),
             pltpu.VMEM((wide // 128, cap * half * blocks, 128), f32),
             pltpu.VMEM((half, cap * half, wide), bf16),
             pltpu.VMEM((half, cap * half, wide), bf16),
             pltpu.VMEM((halves, cap * half * near, 128), f32),
-            pltpu.VMEM((cap, blocks, electrons, orbitals), bf16),
             dma((6,)),
             dma((3,)),
             dma((2,)),
@@ -945,7 +929,23 @@
         compiler_params=pltpu.CompilerParams(
             collective_id=1, has_side_effects=True, vmem_limit_bytes=60 * 1024 * 1024
         ),
-    )(send_walker.reshape(-1), slot_row, fields, walkers, chol_vectors, rotated)
+    )(
+        jnp.transpose(send_walker, (0, 2, 1)).reshape(cap, blocks),
+        slot_row,
+        fields,
+        walkers,
+        chol_vectors,
+        rotated,
+    )
+    return pl.pallas_call(
+        place_kernel,
+        out_shape=(
+            jax.ShapeDtypeStruct(walkers.shape, bf16),
+            jax.ShapeDtypeStruct((slots, nchol), f32),
+        ),
+        in_specs=[smem, vmem, vmem],
+        out_specs=(vmem, vmem),
+    )(slot_row, branch, fb_total)
 
 
 def plan(blocks, walkers, fields, chol_vectors, rotated, send_walker, slot_row):

time: 159 us -> 156 us (0.981)
  local copies, waits for them, and re-layouts: 5.23 us -> 0 us
  Pallas kernels: 153 us -> 155 us
    unnamed x3 -> x0, local copies, waits for them, and re-layouts: 4.63 us -> none
    pallas_call x0 -> x1, Pallas kernels: none -> 2.76 us  [parent_shards(): pl.pallas_call(place_kernel, out_shape=(jax.ShapeDtypeStruct(walkers.shap...]
where the time goes in v4:
time: 156 us
  Pallas kernels  155 us (99%)
    pallas_call x1, Pallas kernels, parent_shards(): pl.pallas_call(functools.partial(parent_kernel, (blocks, cap, rows, elec)...  152 us

profile of v4, /device:TPU:0, one launch (start us, length us, event | category | flops | bytes accessed | tf_op | source)
XLA Modules:
  0.0 155.6 jit_solution(5999005018806435979)
XLA Ops:
  0.6 152.2 %shard_map.77 = (bf16[2,16,64,256]{3,2,1,0:T(8,128)(2,1)}, f32[2,16,1024]{2,1,0:T(8,128)}) custom-call(s32[2,16]{1,0:T(2,128)} %bitcast.3, s32[32]{0:T(128)} %slot_row.3, bf16[32,1024]{1,0:T(8,128)(2,1)} %fields.1, bf16[32,64,256]{2,1,0:T(8,128)(2,1)} %walkers_hbm.1, bf16[1024,16,256]{2,1,0:T(8,128)(2,1)} %chol_hbm.1, bf16[1024,4,256]{2,1,0:T(4,128)(2,1)} %rotated_hbm.1), custom_call_target="tpu_custom_call" | custom-call | tf_op jit(solution)/shard_map/pallas_call | solution.py:877
  152.8 2.8 %shard_map.78 = (bf16[32,64,256]{2,1,0:T(8,128)(2,1)}, f32[32,1024]{1,0:T(8,128)}) custom-call(s32[32]{0:T(128)} %slot_row.3, bf16[2,16,64,256]{3,2,1,0:T(8,128)(2,1)} %get-tuple-element.4.branch, f32[2,16,1024]{2,1,0:T(8,128)} %get-tuple-element.5.fb_total), custom_call_target="tpu_custom_call" | custom-call | tf_op jit(solution)/shard_map/pallas_call | solution.py:940

commit v5 on v4

--- a/solution.py
+++ b/solution.py
@@ -681,6 +681,8 @@
 
         everyone(to_owner)
         nw_recv[c, me] = nw_send[c, me]
+
+    def send_walkers(c):
         mine = pl.ds(pl.multiple_of(side * near, near), near)
 
         def to_slot(d):
@@ -824,6 +826,8 @@
     for c in range(cap):
         wait(op_recv.at[c, pl.ds(0, blocks - 1), pl.ds(1, pairs - 1)], op_got.at[c])
         taylor(c)
+    for c in range(cap):
+        send_walkers(c)
     for c in range(cap):
         wait(nw_recv.at[c, pl.ds(0, blocks - 1)], nw_got.at[c])
         bias(c)

time: 156 us -> 150 us (0.962)
  Pallas kernels: 155 us -> 149 us
    pallas_call x1, Pallas kernels: 152 us -> 146 us  [parent_shards(): pl.pallas_call(functools.partial(parent_kernel, (blocks, cap, rows, elec)...]
where the time goes in v5:
time: 150 us; the launch traced here: 149 us
  Pallas kernels  149 us (99%)
    pallas_call x1, Pallas kernels, parent_shards(): pl.pallas_call(functools.partial(parent_kernel, (blocks, cap, rows, elec)...  146 us

profile of v5, /device:TPU:0, one launch (start us, length us, event | category | flops | bytes accessed | tf_op | source)
XLA Modules:
  0.0 149.3 jit_solution(16639575454966489925)
XLA Ops:
  0.6 145.9 %shard_map.77 = (bf16[2,16,64,256]{3,2,1,0:T(8,128)(2,1)}, f32[2,16,1024]{2,1,0:T(8,128)}) custom-call(s32[2,16]{1,0:T(2,128)} %bitcast.3, s32[32]{0:T(128)} %slot_row.3, bf16[32,1024]{1,0:T(8,128)(2,1)} %fields.1, bf16[32,64,256]{2,1,0:T(8,128)(2,1)} %walkers_hbm.1, bf16[1024,16,256]{2,1,0:T(8,128)(2,1)} %chol_hbm.1, bf16[1024,4,256]{2,1,0:T(4,128)(2,1)} %rotated_hbm.1), custom_call_target="tpu_custom_call" | custom-call | tf_op jit(solution)/shard_map/pallas_call | solution.py:881
  146.5 2.8 %shard_map.78 = (bf16[32,64,256]{2,1,0:T(8,128)(2,1)}, f32[32,1024]{1,0:T(8,128)}) custom-call(s32[32]{0:T(128)} %slot_row.3, bf16[2,16,64,256]{3,2,1,0:T(8,128)(2,1)} %get-tuple-element.4.branch, f32[2,16,1024]{2,1,0:T(8,128)} %get-tuple-element.5.fb_total), custom_call_target="tpu_custom_call" | custom-call | tf_op jit(solution)/shard_map/pallas_call | solution.py:944

commit v6 on v5

--- a/solution.py
+++ b/solution.py
@@ -486,6 +486,15 @@
 
         lax.fori_loop(1, blocks, step, 0)
 
+    def chip_at(k):
+        beyond = across if k < lines else 1 - across
+        return lax.rem(line + k % lines, lines) * 2 + beyond
+
+    def steps_from(o, chip):
+        z, y = chip // 2, lax.rem(chip, 2)
+        apart = y if o // 2 % 2 == 0 else 1 - y
+        return lax.rem(z + lines - o // 4, lines) + apart * lines
+
     def row_of(d):
         return lax.rem(d, 2) * pairs + d // 2
 
@@ -567,7 +576,7 @@
 
     def other_operators(c, first, count):
         for k in range(count):
-            chip = lax.rem(pair + first + k, pairs)
+            chip = chip_at(first + k)
             for q in range(2):
                 low = (k * 2 + q) * blocks
                 at = pl.ds(pl.multiple_of(c * blocks, blocks), blocks)
@@ -595,16 +604,32 @@
     partner = pair * 2 + 1 - core
     beside = (line * 2 + 1 - across) * 2 + core
 
+    bank = lines // 2
+    low_bank = line < bank
+    outer = jnp.where(low_bank, line < bank - 1, line > bank)
+    rank = jnp.where(outer, 1, 0)
+    other_line = jnp.where(low_bank, bank - 1 - line, lines + bank - 1 - line)
+    far_inner = jnp.where(low_bank, bank, bank - 1)
+    far_outer = jnp.where(low_bank, lines - 1, 0)
+    held_lines = (line, other_line, far_inner, far_outer)
+
     def line_at(j):
-        return lax.rem(line + lines - j, lines)
+        return held_lines[j]
+
+    def along(z):
+        return (z * 2 + across) * 2 + core
 
     own, twin = all_fields.at[pair, core], all_fields.at[pair, 1 - core]
     pl.semaphore_wait(barrier, blocks - 1)
     send(own, own, field_send.at[0], field_core.at[0], partner)
-    for j in range(1, lines):
-        peer = (lax.rem(line + j, lines) * 2 + across) * 2 + core
-        send(own, own, field_send.at[2], field_line.at[j], peer)
+    send(own, own, field_send.at[2], field_line.at[2 + rank], along(far_inner))
+    send(own, own, field_send.at[2], field_line.at[1], along(other_line))
     send(own, own, field_send.at[1], field_row.at[0], beside)
+
+    def hand_on(held, j):
+        @pl.when(rank == 0)
+        def _():
+            send(held, held, field_send.at[2], field_line.at[j], along(other_line))
 
     @pl.loop(0, 2)
     def _(t):
@@ -613,6 +638,8 @@
             for j in range(1, lines):
                 held = all_fields.at[line_at(j) * 2 + across, core]
                 wait(held, field_line.at[j])
+                if j > 1:
+                    hand_on(held, j)
                 send(held, held, field_send.at[1], field_row.at[j], beside)
                 send(held, held, field_send.at[0], field_core.at[1], partner)
             wait(twin, field_core.at[0])
@@ -621,18 +648,21 @@
         chip_operators(which)
         send_chip_operators(which)
 
-    for j in range(lines):
-        held = all_fields.at[line_at(j) * 2 + 1 - across, core]
-        wait(held, field_row.at[j])
-        send(held, held, field_send.at[0], field_core.at[1], partner)
-    wait(all_fields.at[pl.ds(0, pairs - 1), 0], field_core.at[1])
-
-    split = pairs // 2
+    wait(all_fields.at[pl.ds(0, lines - 1), 0], field_core.at[1])
 
     @pl.loop(0, cap)
     def _(c):
-        other_operators(c, 1, split)
-        other_operators(c, 1 + split, pairs - 1 - split)
+        other_operators(c, 1, lines - 1)
+
+        @pl.when(c == 0)
+        def _():
+            for j in range(lines):
+                held = all_fields.at[line_at(j) * 2 + 1 - across, core]
+                wait(held, field_row.at[j])
+                send(held, held, field_send.at[0], field_core.at[2], partner)
+            wait(all_fields.at[pl.ds(0, lines), 0], field_core.at[2])
+
+        other_operators(c, lines, lines)
 
     rotated_load.wait()
     turned(rotated_raw, rotated, 0, nchol)
@@ -650,7 +680,7 @@
                 ops.append(
                     jnp.concatenate(
                         [
-                            op_recv[c, o, lax.rem(chip + pairs - o // 2, pairs), q]
+                            op_recv[c, o, steps_from(o, chip), q]
                             for o in range(blocks)
                         ],
                         axis=0,
@@ -841,7 +871,15 @@
 
     wait(all_fields.at[:, 0], field_send.at[0])
     wait(all_fields.at[pl.ds(0, lines), 0], field_send.at[1])
-    wait(all_fields.at[pl.ds(0, lines - 1), 0], field_send.at[2])
+
+    @pl.when(rank == 0)
+    def _():
+        wait(all_fields.at[pl.ds(0, 4), 0], field_send.at[2])
+
+    @pl.when(rank == 1)
+    def _():
+        wait(all_fields.at[pl.ds(0, 2), 0], field_send.at[2])
+
     wait(op_recv.at[:, pl.ds(0, blocks - 1), 0], op_sent.at[cap])
     wait(branch.at[:, pl.ds(0, half - 1 + half // 2)], br_sent.at[0])
     wait(fw_send.at[pl.ds(0, half - 1)], fw_sent.at[0])
@@ -912,7 +950,7 @@
             pltpu.VMEM((halves, cap * half * near, 128), f32),
             dma((6,)),
             dma((3,)),
-            dma((2,)),
+            dma((3,)),
             dma((lines,)),
             dma((lines,)),
             dma((cap + 1,)),
@@ -954,7 +992,7 @@
 
 def plan(blocks, walkers, fields, chol_vectors, rotated, send_walker, slot_row):
     every_entry = blocks * send_walker.shape[-1] == walkers.shape[0]
-    step = parent_shards if every_entry and blocks % 8 == 0 else shards
+    step = parent_shards if every_entry and blocks == 4 * 2 * 2 else shards
     return step(blocks, walkers, fields, chol_vectors, rotated, send_walker, slot_row)
 
 

time: 150 us -> 148 us (0.987)
  no operation moved by 1% of the time
where the time goes in v6:
time: 148 us
  Pallas kernels  148 us (100%)
    pallas_call x1, Pallas kernels, parent_shards(): pl.pallas_call(functools.partial(parent_kernel, (blocks, cap, rows, elec)...  145 us

profile of v6, /device:TPU:0, one launch (start us, length us, event | category | flops | bytes accessed | tf_op | source)
XLA Modules:
  0.0 148.2 jit_solution(12740171737844280711)
XLA Ops:
  0.6 144.8 %shard_map.77 = (bf16[2,16,64,256]{3,2,1,0:T(8,128)(2,1)}, f32[2,16,1024]{2,1,0:T(8,128)}) custom-call(s32[2,16]{1,0:T(2,128)} %bitcast.3, s32[32]{0:T(128)} %slot_row.3, bf16[32,1024]{1,0:T(8,128)(2,1)} %fields.1, bf16[32,64,256]{2,1,0:T(8,128)(2,1)} %walkers_hbm.1, bf16[1024,16,256]{2,1,0:T(8,128)(2,1)} %chol_hbm.1, bf16[1024,4,256]{2,1,0:T(4,128)(2,1)} %rotated_hbm.1), custom_call_target="tpu_custom_call" | custom-call | tf_op jit(solution)/shard_map/pallas_call | solution.py:919
  145.4 2.8 %shard_map.78 = (bf16[32,64,256]{2,1,0:T(8,128)(2,1)}, f32[32,1024]{1,0:T(8,128)}) custom-call(s32[32]{0:T(128)} %slot_row.3, bf16[2,16,64,256]{3,2,1,0:T(8,128)(2,1)} %get-tuple-element.4.branch, f32[2,16,1024]{2,1,0:T(8,128)} %get-tuple-element.5.fb_total), custom_call_target="tpu_custom_call" | custom-call | tf_op jit(solution)/shard_map/pallas_call | solution.py:982

commit v7 on v6

--- a/solution.py
+++ b/solution.py
@@ -540,7 +540,7 @@
 
     scale = field_scale / math.sqrt(nchol)
     cols = rows * orbitals
-    tile = min(1024, cols)
+    tile = min(2048, cols)
     deep = tile // orbitals
 
     def operators(m):

time: 148 us -> 148 us (level)
  no operation moved by 1% of the time
where the time goes in v7:
time: 148 us
  Pallas kernels  147 us (99%)
    pallas_call x1, Pallas kernels, parent_shards(): pl.pallas_call(functools.partial(parent_kernel, (blocks, cap, rows, elec)...  144 us

profile of v7, /device:TPU:0, one launch (start us, length us, event | category | flops | bytes accessed | tf_op | source)
XLA Modules:
  0.0 147.7 jit_solution(16744347326289422406)
XLA Ops:
  0.6 144.3 %shard_map.77 = (bf16[2,16,64,256]{3,2,1,0:T(8,128)(2,1)}, f32[2,16,1024]{2,1,0:T(8,128)}) custom-call(s32[2,16]{1,0:T(2,128)} %bitcast.3, s32[32]{0:T(128)} %slot_row.3, bf16[32,1024]{1,0:T(8,128)(2,1)} %fields.1, bf16[32,64,256]{2,1,0:T(8,128)(2,1)} %walkers_hbm.1, bf16[1024,16,256]{2,1,0:T(8,128)(2,1)} %chol_hbm.1, bf16[1024,4,256]{2,1,0:T(4,128)(2,1)} %rotated_hbm.1), custom_call_target="tpu_custom_call" | custom-call | tf_op jit(solution)/shard_map/pallas_call | solution.py:919
  145.0 2.8 %shard_map.78 = (bf16[32,64,256]{2,1,0:T(8,128)(2,1)}, f32[32,1024]{1,0:T(8,128)}) custom-call(s32[32]{0:T(128)} %slot_row.3, bf16[2,16,64,256]{3,2,1,0:T(8,128)(2,1)} %get-tuple-element.4.branch, f32[2,16,1024]{2,1,0:T(8,128)} %get-tuple-element.5.fb_total), custom_call_target="tpu_custom_call" | custom-call | tf_op jit(solution)/shard_map/pallas_call | solution.py:982

commit v8 on v7

--- a/solution.py
+++ b/solution.py
@@ -861,9 +861,9 @@
     for c in range(cap):
         wait(nw_recv.at[c, pl.ds(0, blocks - 1)], nw_got.at[c])
         bias(c)
+        reduce(c)
         if c == cap - 1:
             forward()
-        reduce(c)
         spread(c)
     collect()
     for c in range(cap):

time: 148 us -> 148 us (level)
  no operation moved by 1% of the time
where the time goes in v8:
time: 148 us
  Pallas kernels  147 us (99%)
    pallas_call x1, Pallas kernels, parent_shards(): pl.pallas_call(functools.partial(parent_kernel, (blocks, cap, rows, elec)...  144 us

profile of v8, /device:TPU:0, one launch (start us, length us, event | category | flops | bytes accessed | tf_op | source)
XLA Modules:
  0.0 147.5 jit_solution(12774562439643246557)
XLA Ops:
  0.6 144.1 %shard_map.77 = (bf16[2,16,64,256]{3,2,1,0:T(8,128)(2,1)}, f32[2,16,1024]{2,1,0:T(8,128)}) custom-call(s32[2,16]{1,0:T(2,128)} %bitcast.3, s32[32]{0:T(128)} %slot_row.3, bf16[32,1024]{1,0:T(8,128)(2,1)} %fields.1, bf16[32,64,256]{2,1,0:T(8,128)(2,1)} %walkers_hbm.1, bf16[1024,16,256]{2,1,0:T(8,128)(2,1)} %chol_hbm.1, bf16[1024,4,256]{2,1,0:T(4,128)(2,1)} %rotated_hbm.1), custom_call_target="tpu_custom_call" | custom-call | tf_op jit(solution)/shard_map/pallas_call | solution.py:919
  144.8 2.8 %shard_map.78 = (bf16[32,64,256]{2,1,0:T(8,128)(2,1)}, f32[32,1024]{1,0:T(8,128)}) custom-call(s32[32]{0:T(128)} %slot_row.3, bf16[2,16,64,256]{3,2,1,0:T(8,128)(2,1)} %get-tuple-element.4.branch, f32[2,16,1024]{2,1,0:T(8,128)} %get-tuple-element.5.fb_total), custom_call_target="tpu_custom_call" | custom-call | tf_op jit(solution)/shard_map/pallas_call | solution.py:982
